TPU v7x, 256 devices: a whole 4x4x8 slice. The times are simulated.
256 devices in a mesh: dp: 16 (over x, y_hi, core), ctx: 16 (over z, y_lo).
Axes of the slice: x: 4, y: 4 (y_hi: 2, y_lo: 2; y = y_hi * 2 + y_lo), z: 8, core: 2. Of those that a mesh axis runs over, the one named last changes fastest.
Arguments:
- query_frames: bfloat16 [65536, 2560], P(('dp', 'ctx')), parts along dimension 0, may hold values from -8 to 8
- key_frames: bfloat16 [65536, 2560], P(('dp', 'ctx')), parts along dimension 0, may hold values from -8 to 8
- value_frames: bfloat16 [65536, 2560], P(('dp', 'ctx')), parts along dimension 0, may hold values from -6 to 6
- stream: bfloat16 [65536, 5120], P(('dp', 'ctx')), parts along dimension 0, may hold values from -1.25 to 1.25
- out_weight: bfloat16 [2560, 5120], P('ctx'), may hold values from -0.125 to 0.125
Outputs:
- layer_out: bfloat16 [65536, 5120], P(('dp', 'ctx')), parts along dimension 0
There are 16 independent parts, one for each index of `dp`. A program takes and returns all parts, laid end to end along the dimension named above; an argument that names none is the same for every part. Nothing has to cross between parts.
All inputs are finite; a program needn't handle non-finite values.
Results may differ from a plain program's by a relative error of at most 0.01.
Values may be sent and summed in bfloat16 or wider, within the bound.
A program may use at most 128 MiB of HBM per device.

v0:
```python
import jax
import jax.numpy as jnp
from jax import lax
from jax.sharding import PartitionSpec as P

HEADS = 20
HEAD_SIZE = 128


def passed_along(value, axis, steps):
    count = lax.axis_size(axis)
    leading, last = (max(0, -steps), min(count, count - steps))
    return lax.ppermute(value, axis, [(source, source + steps) for source in range(leading, last)])


def attend_window(query_block, key_window, value_window, valid):
    block_rows = query_block.shape[0]
    window_rows = key_window.shape[0]
    query_heads = query_block.reshape(block_rows, HEADS, HEAD_SIZE)
    key_heads = key_window.reshape(window_rows, HEADS, HEAD_SIZE)
    value_heads = value_window.reshape(window_rows, HEADS, HEAD_SIZE)
    scores = jnp.einsum(
        "qhd,khd->hqk", query_heads, key_heads, preferred_element_type=jnp.float32
    ) * HEAD_SIZE ** (-0.5)
    scores = jnp.where(valid[None, None, :], scores, -1e30)
    largest = jnp.max(scores, axis=2, keepdims=True)
    expon = jnp.exp(scores - largest)
    probs = (expon / jnp.sum(expon, axis=2, keepdims=True)).astype(jnp.bfloat16)
    context = jnp.einsum("hqk,khd->qhd", probs, value_heads, preferred_element_type=jnp.float32)
    return context.astype(jnp.bfloat16).reshape(block_rows, HEADS * HEAD_SIZE)


def local(query_frames, key_frames, value_frames, stream, out_weight):
    block_rows = query_frames.shape[0]
    position = lax.axis_index("ctx")
    members = lax.axis_size("ctx")
    key_value = jnp.stack([key_frames, value_frames], 0)
    earlier = passed_along(key_value, "ctx", 1)
    later = passed_along(key_value, "ctx", -1)
    window = jnp.concatenate([earlier, key_value, later], 1)
    earlier_ok = jnp.broadcast_to(position > 0, (block_rows,))
    middle_ok = jnp.ones((block_rows,), dtype=bool)
    later_ok = jnp.broadcast_to(position < members - 1, (block_rows,))
    valid = jnp.concatenate([earlier_ok, middle_ok, later_ok])
    context = attend_window(query_frames, window[0], window[1], valid)
    product = jnp.dot(
        context,
        lax.all_gather(out_weight, "ctx", axis=0, tiled=True),
        preferred_element_type=jnp.float32,
    )
    return (stream.astype(jnp.float32) + product).astype(jnp.bfloat16)


def solution(mesh):
    in_specs = (
        P(("dp", "ctx"), None),
        P(("dp", "ctx"), None),
        P(("dp", "ctx"), None),
        P(("dp", "ctx"), None),
        P("ctx", None),
    )
    out_specs = P(("dp", "ctx"), None)
    return jax.shard_map(local, mesh=mesh, in_specs=in_specs, out_specs=out_specs, check_vma=False)
```

profile of v0, /device:TPU:151, one launch (start us, length us, event | category | flops | bytes accessed | tf_op | source)
XLA Modules:
  0.0 679.2 jit_solution(7607029471892932784)
XLA Ops:
  6.5 0.0 all-gather.2.cloned.1.call-start
  6.5 0.7 all-gather.2.cloned.1.call-update
  7.3 1.6 copy.9
  8.9 1.6 copy.10
  10.5 1.7 pad_maximum_fusion.1
  12.2 2.9 collective-permute-start
  15.1 4.5 collective-permute-start.1
  19.6 2.4 copy.11
  22.1 226.5 %collective-permute-done = bf16[2,256,2560]{1,2,0:T(8,128)(2,1)} collective-permute-done((bf16[2,256,2560]{1,2,0:T(8,128)(2,1)}, bf16[2,256,2560]{1,2,0:T(8,128)(2,1)}, u32[]{:S(2)}, u32[]{:S(2)}) %collective-permute-start) | collective-permute-done | bytes 2621472 | tf_op jit(solution)/shard_map/ppermute | solution.py:13
  248.5 9.1 %collective-permute-done.1 = bf16[2,256,2560]{1,2,0:T(8,128)(2,1)} collective-permute-done((bf16[2,256,2560]{1,2,0:T(8,128)(2,1)}, bf16[2,256,2560]{1,2,0:T(8,128)(2,1)}, u32[]{:S(2)}, u32[]{:S(2)}) %collective-permute-start.1) | collective-permute-done | bytes 2621472 | tf_op jit(solution)/shard_map/ppermute | solution.py:13
  257.7 3.4 pad_maximum_fusion
  261.0 0.0 copy-start.1
  261.1 3.3 fusion.15
  264.4 0.0 copy-done.1
  264.4 10.6 %fusion.16 = (f32[20,256]{1,0:T(8,128)S(1)}, f32[20,256,768]{1,2,0:T(8,128)}) fusion(pred[768]{0:T(1024)(128)(4,1)S(1)} %pad_add_fusion, bf16[768,20,128]{0,2,1:T(8,128)(2,1)} %bitcast.31, bf16[256,20,128]{0,2,1:T(8,128)(2,1)S(1)} %bitcast.33), kind=kOutput, calls=%fused_computation.21 | convolution fusion | flops 1022362368 | bytes 20992768 | tf_op jit(solution)/shard_map/sub | solution.py:27
  275.0 0.0 copy-start
  275.0 9.2 %fusion.10 = bf16[20,128,256]{2,1,0:T(8,128)(2,1)} fusion(bf16[768,20,128]{0,2,1:T(8,128)(2,1)} %bitcast.30, f32[20,256,768]{1,2,0:T(8,128)} %get-tuple-element.8, f32[20,256]{1,0:T(8,128)S(1)} %get-tuple-element.7), kind=kOutput, calls=%fused_computation.15 | convolution fusion | flops 1015152640 | bytes 20992000 | tf_op jit(solution)/shard_map/hqk,khd->qhd/dot_general | solution.py:29
  284.2 374.7 %all-gather.2.cloned.1.call-done = bf16[2560,5120]{1,0:T(8,128)(2,1)} async-done(((bf16[160,5120]{1,0:T(8,128)(2,1)}), bf16[2560,5120]{1,0:T(8,128)(2,1)}) %all-gather.2.cloned.1.call-update) | async-done | bytes 26214416 | tf_op jit(solution)/shard_map/all_gather | solution.py:48
  658.9 0.0 copy-done
  658.9 13.5 %fusion.9 = bf16[256,5120]{1,0:T(8,128)(2,1)} fusion(bf16[256,2560]{0,1:T(8,128)(2,1)} %bitcast.32, bf16[2560,5120]{1,0:T(8,128)(2,1)} %all-gather.2.cloned.1.call-done, bf16[256,5120]{1,0:T(8,128)(2,1)S(1)} %copy-done), kind=kOutput, calls=%fused_computation.13 | convolution fusion | flops 6714818560 | bytes 32768000 | tf_op jit(solution)/shard_map/dot_general | solution.py:46
  (4 shorter events, 0.0 us)
Async XLA Ops:
  6.5 652.3 %all-gather.2.cloned.1.call-start = ((), (), s32[]{:S(2)}) async-start(), calls=%async_computation | async-start | bytes 27852800 | tf_op jit(solution)/shard_map/all_gather | solution.py:48
  12.2 236.4 %collective-permute-start = (bf16[2,256,2560]{1,2,0:T(8,128)(2,1)}, bf16[2,256,2560]{1,2,0:T(8,128)(2,1)}, u32[]{:S(2)}, u32[]{:S(2)}) collective-permute-start(bf16[2,256,2560]{1,2,0:T(8,128)(2,1)} %pad_maximum_fusion.1), channel_id=1, source_target_pairs={{0,1},{1,2},{2,3},{3,4},{4,5},{5,6},{6,7},{7,8},{8,9},{9,10},{10,1... | collective-permute-start | bytes 7864328 | tf_op jit(solution)/shard_map/ppermute | solution.py:13
  15.1 242.6 %collective-permute-start.1 = (bf16[2,256,2560]{1,2,0:T(8,128)(2,1)}, bf16[2,256,2560]{1,2,0:T(8,128)(2,1)}, u32[]{:S(2)}, u32[]{:S(2)}) collective-permute-start(bf16[2,256,2560]{1,2,0:T(8,128)(2,1)} %pad_maximum_fusion.1), channel_id=1, source_target_pairs={{1,0},{2,1},{3,2},{4,3},{5,4},{6,5},{7,6},{8,7},{9,8},{10,9},{11,1... | collective-permute-start | bytes 7864328 | tf_op jit(solution)/shard_map/ppermute | solution.py:13
  261.0 3.3 copy-start.1
  275.0 383.9 %copy-start = (bf16[256,5120]{1,0:T(8,128)(2,1)S(1)}, bf16[256,5120]{1,0:T(8,128)(2,1)}, u32[]{:S(2)}) copy-start(bf16[256,5120]{1,0:T(8,128)(2,1)} %param.8) | copy-start | bytes 7864324
Sparse Core Ops, SparseCore 0:
  9.1 649.7 all-gather.1
where the time goes:
time: 679 us
  waiting for transfers between devices  611 us (90%)
  matrix products  33.3 us (5%)
  between operations  13.5 us (2%)
  local copies, waits for them, and re-layouts  8.97 us (1%)
  starting transfers between devices  7.39 us (1%)
    all_gather x1, waiting for transfers between devices, local(): lax.all_gather(out_weight, 'ctx', axis=0, tiled=True)  375 us
    ppermute x2, waiting for transfers between devices, passed_along(): lax.ppermute(value, axis, [(source, source + steps) for source in range(l...  236 us
  transfers between devices with their start and end apart: 3, of which 3 were waited for; matrix products, arithmetic and copies ran while one was open for 5% of the time, Pallas kernels for 0%

commit v1 on v0

--- a/solution.py
+++ b/solution.py
@@ -45,7 +45,9 @@
     context = attend_window(query_frames, window[0], window[1], valid)
     product = jnp.dot(
         context,
-        lax.all_gather(out_weight, "ctx", axis=0, tiled=True),
+        jnp.concatenate(
+            lax.all_to_all(jnp.stack([out_weight] * lax.axis_size("ctx")), "ctx", 0, 0), axis=0
+        ),
         preferred_element_type=jnp.float32,
     )
     return (stream.astype(jnp.float32) + product).astype(jnp.bfloat16)

time: 679 us -> 719 us (1.059)
  the two profiles are of different devices: /device:TPU:151 before, /device:TPU:162 now
where the time goes in v1:
time: 719 us
  waiting for transfers between devices  648 us (90%)
  matrix products  33.3 us (5%)
  local copies, waits for them, and re-layouts  17.8 us (2%)
  starting transfers between devices  14.1 us (2%)
    ppermute x2, waiting for transfers between devices, passed_along(): lax.ppermute(value, axis, [(source, source + steps) for source in range(l...  648 us
  transfers between devices with their start and end apart: 3, of which 2 were waited for; matrix products, arithmetic and copies ran while one was open for 5% of the time, Pallas kernels for 0%

profile of v1, /device:TPU:162, one launch (start us, length us, event | category | flops | bytes accessed | tf_op | source)
XLA Modules:
  0.0 718.6 jit_solution(11127357772661774270)
XLA Ops:
  0.0 9.7 %stack.11 = bf16[16,160,5120]{2,1,0:T(8,128)(2,1)} broadcast(bf16[160,5120]{1,0:T(8,128)(2,1)} %param.9), dimensions={1,2} | broadcast | bytes 27852800 | tf_op jit(solution)/shard_map/stack | solution.py:49
  9.7 0.0 copy-start.1
  9.7 7.9 %all-to-all-start = ((bf16[16,160,5120]{2,1,0:T(8,128)(2,1)}), bf16[16,160,5120]{2,1,0:T(8,128)(2,1)}, u32[]{:S(2)}, u32[]{:S(2)}) async-start(bf16[16,160,5120]{2,1,0:T(8,128)(2,1)} %stack.11), calls=%async_computation | async-start | bytes 52428800 | tf_op jit(solution)/shard_map/all_to_all | solution.py:49
  17.6 0.0 copy-done.1
  17.6 0.6 copy.9
  18.2 1.6 copy.10
  19.8 1.7 pad_maximum_fusion.1
  21.6 4.3 collective-permute-start.1
  25.8 1.9 collective-permute-start
  27.8 2.5 copy.11
  30.3 625.2 %collective-permute-done.1 = bf16[2,256,2560]{1,2,0:T(8,128)(2,1)} collective-permute-done((bf16[2,256,2560]{1,2,0:T(8,128)(2,1)}, bf16[2,256,2560]{1,2,0:T(8,128)(2,1)}, u32[]{:S(2)}, u32[]{:S(2)}) %collective-permute-start.1) | collective-permute-done | bytes 2621472 | tf_op jit(solution)/shard_map/ppermute | solution.py:13
  655.4 23.1 %collective-permute-done = bf16[2,256,2560]{1,2,0:T(8,128)(2,1)} collective-permute-done((bf16[2,256,2560]{1,2,0:T(8,128)(2,1)}, bf16[2,256,2560]{1,2,0:T(8,128)(2,1)}, u32[]{:S(2)}, u32[]{:S(2)}) %collective-permute-start) | collective-permute-done | bytes 2621472 | tf_op jit(solution)/shard_map/ppermute | solution.py:13
  678.5 3.3 pad_maximum_fusion
  681.8 0.0 copy-start.2
  681.8 3.4 fusion.15
  685.3 0.0 copy-done.2
  685.3 10.6 %fusion.16 = (f32[20,256]{1,0:T(8,128)S(1)}, f32[20,256,768]{1,2,0:T(8,128)}) fusion(pred[768]{0:T(1024)(128)(4,1)S(1)} %pad_add_fusion, bf16[768,20,128]{0,2,1:T(8,128)(2,1)} %bitcast.32, bf16[256,20,128]{0,2,1:T(8,128)(2,1)S(1)} %bitcast.34), kind=kOutput, calls=%fused_computation.21 | convolution fusion | flops 1022362368 | bytes 20992768 | tf_op jit(solution)/shard_map/sub | solution.py:27
  695.9 0.0 copy-start
  695.9 9.2 %fusion.10 = bf16[20,128,256]{2,1,0:T(8,128)(2,1)} fusion(bf16[768,20,128]{0,2,1:T(8,128)(2,1)} %bitcast.31, f32[20,256,768]{1,2,0:T(8,128)} %get-tuple-element.8, f32[20,256]{1,0:T(8,128)S(1)} %get-tuple-element.7), kind=kOutput, calls=%fused_computation.15 | convolution fusion | flops 1015152640 | bytes 20992000 | tf_op jit(solution)/shard_map/hqk,khd->qhd/dot_general | solution.py:29
  705.1 0.0 all-to-all-done
  705.1 0.0 copy-done
  705.1 13.5 %fusion.9 = bf16[256,5120]{1,0:T(8,128)(2,1)} fusion(bf16[256,2560]{0,1:T(8,128)(2,1)} %bitcast.33, bf16[2560,5120]{1,0:T(8,128)(2,1)} %bitcast.8, bf16[256,5120]{1,0:T(8,128)(2,1)S(1)} %copy-done), kind=kOutput, calls=%fused_computation.13 | convolution fusion | flops 6714818560 | bytes 32768000 | tf_op jit(solution)/shard_map/dot_general | solution.py:46
  (4 shorter events, 0.0 us)
Async XLA Ops:
  9.7 7.9 %copy-start.1 = (bf16[256,2560]{1,0:T(8,128)(2,1)S(1)}, bf16[256,2560]{1,0:T(8,128)(2,1)}, u32[]{:S(2)}) copy-start(bf16[256,2560]{1,0:T(8,128)(2,1)} %param.6) | copy-start | bytes 3932164
  9.7 695.4 %all-to-all-start = ((bf16[16,160,5120]{2,1,0:T(8,128)(2,1)}), bf16[16,160,5120]{2,1,0:T(8,128)(2,1)}, u32[]{:S(2)}, u32[]{:S(2)}) async-start(bf16[16,160,5120]{2,1,0:T(8,128)(2,1)} %stack.11), calls=%async_computation | async-start | bytes 52428800 | tf_op jit(solution)/shard_map/all_to_all | solution.py:49
  21.6 633.9 %collective-permute-start.1 = (bf16[2,256,2560]{1,2,0:T(8,128)(2,1)}, bf16[2,256,2560]{1,2,0:T(8,128)(2,1)}, u32[]{:S(2)}, u32[]{:S(2)}) collective-permute-start(bf16[2,256,2560]{1,2,0:T(8,128)(2,1)} %pad_maximum_fusion.1), channel_id=1, source_target_pairs={{1,0},{2,1},{3,2},{4,3},{5,4},{6,5},{7,6},{8,7},{9,8},{10,9},{11,1... | collective-permute-start | bytes 7864328 | tf_op jit(solution)/shard_map/ppermute | solution.py:13
  25.8 652.7 %collective-permute-start = (bf16[2,256,2560]{1,2,0:T(8,128)(2,1)}, bf16[2,256,2560]{1,2,0:T(8,128)(2,1)}, u32[]{:S(2)}, u32[]{:S(2)}) collective-permute-start(bf16[2,256,2560]{1,2,0:T(8,128)(2,1)} %pad_maximum_fusion.1), channel_id=1, source_target_pairs={{0,1},{1,2},{2,3},{3,4},{4,5},{5,6},{6,7},{7,8},{8,9},{9,10},{10,1... | collective-permute-start | bytes 7864328 | tf_op jit(solution)/shard_map/ppermute | solution.py:13
  681.8 3.4 copy-start.2
  695.9 9.2 %copy-start = (bf16[256,5120]{1,0:T(8,128)(2,1)S(1)}, bf16[256,5120]{1,0:T(8,128)(2,1)}, u32[]{:S(2)}) copy-start(bf16[256,5120]{1,0:T(8,128)(2,1)} %param.8) | copy-start | bytes 7864324
